TPU v7x, 32 devices: a whole 2x2x4 slice. The times are simulated.
32 devices in a mesh: ctx: 16 (over z, y, core), fsdp: 2 (over x).
Axes of the slice: x: 2, y: 2, z: 4, core: 2. Of those that a mesh axis runs over, the one named last changes fastest.
Arguments:
- layer_input: float32 [4096, 1024], P(('ctx', 'fsdp')), may hold values from -6 to 6
- grad_output: float32 [4096, 1024], P(('ctx', 'fsdp')), may hold values from -6 to 6
- positions: int32 [4096], replicated, may hold values from 0 to 4095, as said below
- w_query: bfloat16 [1024, 2048], P(('ctx', 'fsdp')), may hold values from -0.1875 to 0.1875
- w_key: bfloat16 [1024, 2048], P(('ctx', 'fsdp')), may hold values from -0.1875 to 0.1875
- w_value: bfloat16 [1024, 2048], P(('ctx', 'fsdp')), may hold values from -0.1875 to 0.1875
- w_out: bfloat16 [2048, 1024], P(('ctx', 'fsdp')), may hold values from -0.125 to 0.125
- w_gate: bfloat16 [1024, 4096], P(('ctx', 'fsdp')), may hold values from -0.1875 to 0.1875
- w_up: bfloat16 [1024, 4096], P(('ctx', 'fsdp')), may hold values from -0.1875 to 0.1875
- w_down: bfloat16 [4096, 1024], P(('ctx', 'fsdp')), may hold values from -0.09375 to 0.09375
- gain_query: bfloat16 [2048], P(('ctx', 'fsdp')), may hold values from 0.5 to 1.5
- gain_key: bfloat16 [2048], P(('ctx', 'fsdp')), may hold values from 0.5 to 1.5
- gain_attn: bfloat16 [1024], P(('ctx', 'fsdp')), may hold values from 0.5 to 1.5
- gain_mlp: bfloat16 [1024], P(('ctx', 'fsdp')), may hold values from 0.5 to 1.5
Outputs:
- output: float32 [4096, 1024], P(('ctx', 'fsdp'))
- grad_input: float32 [4096, 1024], P(('ctx', 'fsdp'))
- grad_w_query: float32 [1024, 2048], P('fsdp')
- grad_w_key: float32 [1024, 2048], P('fsdp')
- grad_w_value: float32 [1024, 2048], P('fsdp')
- grad_w_out: float32 [2048, 1024], P('fsdp')
- grad_w_gate: float32 [1024, 4096], P('fsdp')
- grad_w_up: float32 [1024, 4096], P('fsdp')
- grad_w_down: float32 [4096, 1024], P('fsdp')
- grad_gain_query: float32 [2048], P('fsdp')
- grad_gain_key: float32 [2048], P('fsdp')
- grad_gain_attn: float32 [1024], P('fsdp')
- grad_gain_mlp: float32 [1024], P('fsdp')
Inputs may be any that keep to these rules, and one draw needn't show every extreme that they name: positions holds each of 0 to 4095 once. The 128 rows of device d (rows d * 128 onward, devices in the order ctx then fsdp) are two sequence blocks of 64 consecutive positions: block p first and block 63 - p second, for some p below 32 that differs from device to device.
All inputs are finite; a program needn't handle non-finite values.
Results may differ from a plain program's by a relative error of at most 0.023.
Values may be sent and summed in bfloat16 or wider, within the bound.
No kernel may reach another device: no remote copies, remote signals or barrier semaphores. Data moves between devices by JAX's collectives and lax.ppermute only.
A program may use at most 768 MiB of HBM per device.

v0:
```python
import math
import jax
import jax.numpy as jnp
from jax import lax
from jax.sharding import PartitionSpec as P

H = 16
HD = 128
EPS = 1e-06
THETA = 500000.0
NEG = -1e30


def norm_forward(value, gain):
    recip = lax.rsqrt(jnp.mean(value * value, axis=-1, keepdims=True) + EPS)
    return (value * recip * gain.astype(jnp.float32), recip)


def norm_backward(value, recip, gain, grad_out):
    scaled = grad_out * gain.astype(jnp.float32)
    width = value.shape[-1]
    grad_in = (
        recip * scaled
        - value * (recip * recip * recip) * jnp.sum(scaled * value, axis=-1, keepdims=True) / width
    )
    grad_gain = jnp.sum(grad_out * value * recip, axis=0)
    return (grad_in, grad_gain)


def rotary_tables(where, head_size):
    half = head_size // 2
    freqs = THETA ** (-(2.0 * jnp.arange(half, dtype=jnp.float32)) / head_size)
    angles = where.astype(jnp.float32)[:, None] * freqs[None, :]
    return (jnp.cos(angles)[:, None, :], jnp.sin(angles)[:, None, :])


def rotate(flat, cosine, sine, heads, head_size):
    half = head_size // 2
    table = flat.reshape(flat.shape[0], heads, head_size)
    first = table[..., :half]
    second = table[..., half:]
    joined = jnp.concatenate(
        [first * cosine - second * sine, second * cosine + first * sine], axis=-1
    )
    return joined.reshape(flat.shape[0], heads * head_size)


def unrotate(flat, cosine, sine, heads, head_size):
    half = head_size // 2
    table = flat.reshape(flat.shape[0], heads, head_size)
    first = table[..., :half]
    second = table[..., half:]
    joined = jnp.concatenate(
        [first * cosine + second * sine, second * cosine - first * sine], axis=-1
    )
    return joined.reshape(flat.shape[0], heads * head_size)


def block_size():
    return 512


def per_device(
    layer_input,
    grad_output,
    positions,
    w_query,
    w_key,
    w_value,
    w_out,
    w_gate,
    w_up,
    w_down,
    gain_query,
    gain_key,
    gain_attn,
    gain_mlp,
):
    f32 = jnp.float32
    bf16 = jnp.bfloat16
    rows = layer_input.shape[0]
    heads = H
    head_size = HD
    width = heads * head_size
    scale = 1.0 / math.sqrt(head_size)
    first_row = lax.axis_index(("ctx", "fsdp")) * rows
    my_pos = lax.dynamic_slice_in_dim(positions, first_row, rows)
    cosine, sine = rotary_tables(my_pos, head_size)
    full_query, full_key, full_value, full_out, full_gq, full_gk, full_ga = (
        lax.all_gather(w_query, ("ctx", "fsdp"), axis=0, tiled=True),
        lax.all_gather(w_key, ("ctx", "fsdp"), axis=0, tiled=True),
        lax.all_gather(w_value, ("ctx", "fsdp"), axis=0, tiled=True),
        lax.all_gather(w_out, ("ctx", "fsdp"), axis=0, tiled=True),
        lax.all_gather(gain_query, ("ctx", "fsdp"), axis=0, tiled=True),
        lax.all_gather(gain_key, ("ctx", "fsdp"), axis=0, tiled=True),
        lax.all_gather(gain_attn, ("ctx", "fsdp"), axis=0, tiled=True),
    )
    xb = layer_input.astype(bf16)
    query_pre = jnp.dot(xb, full_query, preferred_element_type=f32)
    key_pre = jnp.dot(xb, full_key, preferred_element_type=f32)
    query_normed, q_recip = norm_forward(query_pre, full_gq)
    key_normed, k_recip = norm_forward(key_pre, full_gk)
    query = rotate(query_normed, cosine, sine, heads, head_size).astype(bf16)
    key = rotate(key_normed, cosine, sine, heads, head_size).astype(bf16)
    value = jnp.dot(xb, full_value, preferred_element_type=f32).astype(bf16)
    q3 = query.reshape(rows, heads, head_size)
    k3 = key.reshape(rows, heads, head_size)
    v3 = value.reshape(rows, heads, head_size)
    start_state = (
        jnp.full((heads, rows), NEG, f32),
        jnp.zeros((heads, rows), f32),
        jnp.zeros((rows, heads, head_size), f32),
    )
    keys_in = lax.all_gather(key, ("ctx", "fsdp"), axis=0, tiled=True)
    values_in = lax.all_gather(value, ("ctx", "fsdp"), axis=0, tiled=True)
    count = keys_in.shape[0]
    size = block_size()

    def attend_step(state, index):
        top_run, total_run, accum = state
        low = index * size
        kb = lax.dynamic_slice_in_dim(keys_in, low, size).reshape(size, heads, head_size)
        vb = lax.dynamic_slice_in_dim(values_in, low, size).reshape(size, heads, head_size)
        pb = lax.dynamic_slice_in_dim(positions, low, size)
        scores = jnp.einsum("qhd,khd->hqk", q3, kb, preferred_element_type=f32) * scale
        allowed = pb[None, None, :] <= my_pos[None, :, None]
        scores = jnp.where(allowed, scores, NEG)
        top_new = jnp.maximum(top_run, jnp.max(scores, axis=-1))
        probs = jnp.where(allowed, jnp.exp(scores - top_new[:, :, None]), 0.0)
        factor = jnp.exp(top_run - top_new)
        total_new = total_run * factor + jnp.sum(probs, axis=-1)
        accum_new = accum * factor.T[:, :, None] + jnp.einsum(
            "hqk,khd->qhd", probs.astype(bf16), vb, preferred_element_type=f32
        )
        return ((top_new, total_new, accum_new), None)

    state, _ = lax.scan(attend_step, start_state, jnp.arange(count // size, dtype=jnp.int32))
    top_run, total_run, accum = state
    lse = top_run + jnp.log(total_run)
    attended = (accum / total_run.T[:, :, None]).reshape(rows, width).astype(bf16)
    full_gate, full_up, full_down, full_gm = (
        lax.all_gather(w_gate, ("ctx", "fsdp"), axis=0, tiled=True),
        lax.all_gather(w_up, ("ctx", "fsdp"), axis=0, tiled=True),
        lax.all_gather(w_down, ("ctx", "fsdp"), axis=0, tiled=True),
        lax.all_gather(gain_mlp, ("ctx", "fsdp"), axis=0, tiled=True),
    )
    proj = jnp.dot(attended, full_out, preferred_element_type=f32)
    attn_branch, a_recip = norm_forward(proj, full_ga)
    mid = layer_input + attn_branch
    midb = mid.astype(bf16)
    gate = jnp.dot(midb, full_gate, preferred_element_type=f32)
    up = jnp.dot(midb, full_up, preferred_element_type=f32)
    sig = jax.nn.sigmoid(gate)
    silu = gate * sig
    hidden = (silu * up).astype(bf16)
    down = jnp.dot(hidden, full_down, preferred_element_type=f32)
    mlp_branch, m_recip = norm_forward(down, full_gm)
    output = mid + mlp_branch
    d_down_f, local_gm = norm_backward(down, m_recip, full_gm, grad_output)
    d_down = d_down_f.astype(bf16)
    local_wd = jnp.dot(hidden.T, d_down, preferred_element_type=f32)
    d_hidden = jnp.dot(d_down, full_down.T, preferred_element_type=f32)
    d_gate = (d_hidden * up * sig * (1.0 + gate * (1.0 - sig))).astype(bf16)
    d_up = (d_hidden * silu).astype(bf16)
    local_wg = jnp.dot(midb.T, d_gate, preferred_element_type=f32)
    local_wu = jnp.dot(midb.T, d_up, preferred_element_type=f32)
    d_mid = (
        grad_output
        + jnp.dot(d_gate, full_gate.T, preferred_element_type=f32)
        + jnp.dot(d_up, full_up.T, preferred_element_type=f32)
    )
    d_proj_f, local_ga = norm_backward(proj, a_recip, full_ga, d_mid)
    d_proj = d_proj_f.astype(bf16)
    local_wo = jnp.dot(attended.T, d_proj, preferred_element_type=f32)
    d_att = jnp.dot(d_proj, full_out.T, preferred_element_type=f32).astype(bf16)
    da3 = d_att.reshape(rows, heads, head_size)
    delta_rows = jnp.sum(
        da3.astype(f32) * attended.reshape(rows, heads, head_size).astype(f32), axis=-1
    )
    delta_local = delta_rows.T
    lse_all, delta_all = (
        lax.all_gather(lse.T, ("ctx", "fsdp"), axis=0, tiled=True),
        lax.all_gather(delta_rows, ("ctx", "fsdp"), axis=0, tiled=True),
    )
    zero_rows = jnp.zeros((rows, heads, head_size), f32)
    query_keys_in = lax.all_gather(key, ("ctx", "fsdp"), axis=0, tiled=True)
    query_values_in = lax.all_gather(value, ("ctx", "fsdp"), axis=0, tiled=True)
    count = query_keys_in.shape[0]
    query_size = block_size()

    def query_step(accum, index):
        low = index * query_size
        kb = lax.dynamic_slice_in_dim(query_keys_in, low, query_size).reshape(
            query_size, heads, head_size
        )
        vb = lax.dynamic_slice_in_dim(query_values_in, low, query_size).reshape(
            query_size, heads, head_size
        )
        pb = lax.dynamic_slice_in_dim(positions, low, query_size)
        scores = jnp.einsum("qhd,khd->hqk", q3, kb, preferred_element_type=f32) * scale
        allowed = pb[None, None, :] <= my_pos[None, :, None]
        probs = jnp.where(allowed, jnp.exp(scores - lse[:, :, None]), 0.0)
        dprob = jnp.einsum("qhd,khd->hqk", da3, vb, preferred_element_type=f32)
        dscore = (probs * (dprob - delta_local[:, :, None])).astype(bf16)
        return (accum + jnp.einsum("hqk,khd->qhd", dscore, kb, preferred_element_type=f32), None)

    accum, _ = lax.scan(query_step, zero_rows, jnp.arange(count // query_size, dtype=jnp.int32))
    queries_in = lax.all_gather(query, ("ctx", "fsdp"), axis=0, tiled=True)
    cotangents_in = lax.all_gather(d_att, ("ctx", "fsdp"), axis=0, tiled=True)
    count = queries_in.shape[0]
    key_size = block_size()

    def key_step(state, index):
        dk_run, dv_run = state
        low = index * key_size
        qb = lax.dynamic_slice_in_dim(queries_in, low, key_size).reshape(key_size, heads, head_size)
        db = lax.dynamic_slice_in_dim(cotangents_in, low, key_size).reshape(
            key_size, heads, head_size
        )
        pb = lax.dynamic_slice_in_dim(positions, low, key_size)
        lse_b = lax.dynamic_slice_in_dim(lse_all, low, key_size)
        delta_b = lax.dynamic_slice_in_dim(delta_all, low, key_size)
        scores = jnp.einsum("qhd,khd->hqk", qb, k3, preferred_element_type=f32) * scale
        allowed = my_pos[None, None, :] <= pb[None, :, None]
        probs = jnp.where(allowed, jnp.exp(scores - lse_b.T[:, :, None]), 0.0)
        dv_new = dv_run + jnp.einsum(
            "hqk,qhd->khd", probs.astype(bf16), db, preferred_element_type=f32
        )
        dprob = jnp.einsum("qhd,khd->hqk", db, v3, preferred_element_type=f32)
        dscore = (probs * (dprob - delta_b.T[:, :, None])).astype(bf16)
        dk_new = dk_run + jnp.einsum("hqk,qhd->khd", dscore, qb, preferred_element_type=f32)
        return ((dk_new, dv_new), None)

    state, _ = lax.scan(
        key_step, (zero_rows, zero_rows), jnp.arange(count // key_size, dtype=jnp.int32)
    )
    dk_acc, dv_acc = state
    d_query_rot = (accum * scale).reshape(rows, width)
    d_key_rot = (dk_acc * scale).reshape(rows, width)
    d_value = dv_acc.reshape(rows, width).astype(bf16)
    dq_f, local_gq = norm_backward(
        query_pre, q_recip, full_gq, unrotate(d_query_rot, cosine, sine, heads, head_size)
    )
    dk_f, local_gk = norm_backward(
        key_pre, k_recip, full_gk, unrotate(d_key_rot, cosine, sine, heads, head_size)
    )
    d_query_pre = dq_f.astype(bf16)
    d_key_pre = dk_f.astype(bf16)
    local_wq = jnp.dot(xb.T, d_query_pre, preferred_element_type=f32)
    local_wk = jnp.dot(xb.T, d_key_pre, preferred_element_type=f32)
    local_wv = jnp.dot(xb.T, d_value, preferred_element_type=f32)
    grad_input = (
        d_mid
        + jnp.dot(d_query_pre, full_query.T, preferred_element_type=f32)
        + jnp.dot(d_key_pre, full_key.T, preferred_element_type=f32)
        + jnp.dot(d_value, full_value.T, preferred_element_type=f32)
    )
    (
        share_wq,
        share_wk,
        share_wv,
        share_wo,
        share_wg,
        share_wu,
        share_wd,
        share_gq,
        share_gk,
        share_ga,
        share_gm,
    ) = (
        lax.psum_scatter(
            local_wq.astype(jnp.bfloat16), "fsdp", scatter_dimension=0, tiled=True
        ).astype(jnp.float32),
        lax.psum_scatter(
            local_wk.astype(jnp.bfloat16), "fsdp", scatter_dimension=0, tiled=True
        ).astype(jnp.float32),
        lax.psum_scatter(
            local_wv.astype(jnp.bfloat16), "fsdp", scatter_dimension=0, tiled=True
        ).astype(jnp.float32),
        lax.psum_scatter(
            local_wo.astype(jnp.bfloat16), "fsdp", scatter_dimension=0, tiled=True
        ).astype(jnp.float32),
        lax.psum_scatter(
            local_wg.astype(jnp.bfloat16), "fsdp", scatter_dimension=0, tiled=True
        ).astype(jnp.float32),
        lax.psum_scatter(
            local_wu.astype(jnp.bfloat16), "fsdp", scatter_dimension=0, tiled=True
        ).astype(jnp.float32),
        lax.psum_scatter(
            local_wd.astype(jnp.bfloat16), "fsdp", scatter_dimension=0, tiled=True
        ).astype(jnp.float32),
        lax.psum_scatter(
            local_gq.astype(jnp.bfloat16), "fsdp", scatter_dimension=0, tiled=True
        ).astype(jnp.float32),
        lax.psum_scatter(
            local_gk.astype(jnp.bfloat16), "fsdp", scatter_dimension=0, tiled=True
        ).astype(jnp.float32),
        lax.psum_scatter(
            local_ga.astype(jnp.bfloat16), "fsdp", scatter_dimension=0, tiled=True
        ).astype(jnp.float32),
        lax.psum_scatter(
            local_gm.astype(jnp.bfloat16), "fsdp", scatter_dimension=0, tiled=True
        ).astype(jnp.float32),
    )
    (
        total_wq,
        total_wk,
        total_wv,
        total_wo,
        total_wg,
        total_wu,
        total_wd,
        total_gq,
        total_gk,
        total_ga,
        total_gm,
    ) = lax.psum(
        (
            share_wq,
            share_wk,
            share_wv,
            share_wo,
            share_wg,
            share_wu,
            share_wd,
            share_gq,
            share_gk,
            share_ga,
            share_gm,
        ),
        "ctx",
    )
    return (
        output,
        grad_input,
        total_wq,
        total_wk,
        total_wv,
        total_wo,
        total_wg,
        total_wu,
        total_wd,
        total_gq,
        total_gk,
        total_ga,
        total_gm,
    )


def solution(mesh):
    in_specs = (
        P(("ctx", "fsdp"), None),
        P(("ctx", "fsdp"), None),
        P(),
        P(("ctx", "fsdp"), None),
        P(("ctx", "fsdp"), None),
        P(("ctx", "fsdp"), None),
        P(("ctx", "fsdp"), None),
        P(("ctx", "fsdp"), None),
        P(("ctx", "fsdp"), None),
        P(("ctx", "fsdp"), None),
        P(("ctx", "fsdp")),
        P(("ctx", "fsdp")),
        P(("ctx", "fsdp")),
        P(("ctx", "fsdp")),
    )
    out_specs = (
        P(("ctx", "fsdp"), None),
        P(("ctx", "fsdp"), None),
        P("fsdp", None),
        P("fsdp", None),
        P("fsdp", None),
        P("fsdp", None),
        P("fsdp", None),
        P("fsdp", None),
        P("fsdp", None),
        P("fsdp"),
        P("fsdp"),
        P("fsdp"),
        P("fsdp"),
    )
    return jax.shard_map(
        per_device, mesh=mesh, in_specs=in_specs, out_specs=out_specs, check_vma=False
    )
```

profile of v0, /device:TPU:20, one launch (start us, length us, event | category | flops | bytes accessed | tf_op | source)
XLA Modules:
  0.0 2494.5 jit_solution(6300280929021746939)
XLA Ops:
  10.6 62.4 %all-gather.18.cloned.1.call-done = bf16[1024,2048]{1,0:T(8,128)(2,1)} async-done(((bf16[32,2048]{1,0:T(8,128)(2,1)}), bf16[1024,2048]{1,0:T(8,128)(2,1)}) %all-gather.18.cloned.1.call-update) | async-done | bytes 4194320 | tf_op jit(solution)/shard_map/all_gather | solution.py:92
  77.8 40.0 %all-reduce.9 = (bf16[2048]{0:T(1024)(128)(2,1)S(1)}, bf16[2048]{0:T(1024)(128)(2,1)S(1)}, bf16[1024]{0:T(1024)(128)(2,1)S(1)}, bf16[1024]{0:T(1024)(128)(2,1)S(1)}) all-reduce(bf16[2048]{0:T(1024)(128)(2,1)S(1)} %dynamic-update-slice, bf16[2048]{0:T(1024)(128)(2,1)S(1)} %dynamic-update-slice.1, ...), channel_id=1, replica_groups=mesh['ctx'=16,'fsdp'=2] {'ctx','fsdp'}, use_global_device_ids=true, to_apply=%add | all-reduce | flops 6144 | bytes 24576
  118.9 17.7 all-gather.12.cloned.1.call-done
  141.2 59.0 %all-gather.16.cloned.1.call-done = bf16[1024,2048]{1,0:T(8,128)(2,1)} async-done(((bf16[32,2048]{1,0:T(8,128)(2,1)}), bf16[1024,2048]{1,0:T(8,128)(2,1)}) %all-gather.16.cloned.1.call-update) | async-done | bytes 4194320 | tf_op jit(solution)/shard_map/all_gather | solution.py:90
  211.3 104.9 %all-gather.20.cloned.1.call-done = bf16[4096,2048]{1,0:T(8,128)(2,1)} async-done(((bf16[128,2048]{1,0:T(8,128)(2,1)}), bf16[4096,2048]{1,0:T(8,128)(2,1)}) %all-gather.20.cloned.1.call-update) | async-done | bytes 16777232 | tf_op jit(solution)/shard_map/all_gather | solution.py:115
  316.1 20.8 copy.105
  336.9 127.5 %all-gather.14.cloned.1.call-done = bf16[4096,2048]{0,1:T(8,128)(2,1)} async-done(((bf16[128,2048]{0,1:T(8,128)(2,1)}), bf16[4096,2048]{0,1:T(8,128)(2,1)}) %all-gather.14.cloned.1.call-update) | async-done | bytes 16777232 | tf_op jit(solution)/shard_map/all_gather | solution.py:114
  464.5 110.7 %while.39 = (s32[]{:T(128)}, f32[16,128]{1,0:T(8,128)S(1)}, f32[16,128]{1,0:T(8,128)S(1)}, f32[128,16,128]{0,2,1:T(8,128)}, s32[8]{0:T(128)S(1)}, /*index=5*/s32...) while((s32[]{:T(128)}, f32[16,128]{1,0:T(8,128)S(1)}, ...), condition=%wide.region_5.6_spmd.clone, body=%wide.region_2.5_spmd.clone.sunk | while | flops 551366656 | bytes 44964588 | solution.py:137
  580.7 25.8 %all-gather.24.cloned.1.call-done = bf16[1024,4096]{1,0:T(8,128)(2,1)} async-done(((bf16[32,4096]{1,0:T(8,128)(2,1)}), bf16[1024,4096]{1,0:T(8,128)(2,1)}) %all-gather.24.cloned.1.call-update) | async-done | bytes 8388624 | tf_op jit(solution)/shard_map/all_gather | solution.py:142
  606.5 6.0 fusion.48
  612.5 72.7 %all-gather.26.cloned.1.call-done = bf16[1024,4096]{1,0:T(8,128)(2,1)} async-done(((bf16[32,4096]{1,0:T(8,128)(2,1)}), bf16[1024,4096]{1,0:T(8,128)(2,1)}) %all-gather.26.cloned.1.call-update) | async-done | bytes 8388624 | tf_op jit(solution)/shard_map/all_gather | solution.py:143
  685.3 6.9 multiply_convert_fusion.3
  692.1 71.9 %all-gather.28.cloned.1.call-done = bf16[4096,1024]{1,0:T(8,128)(2,1)} async-done(((bf16[128,1024]{1,0:T(8,128)(2,1)}), bf16[4096,1024]{1,0:T(8,128)(2,1)}) %all-gather.28.cloned.1.call-update) | async-done | bytes 8388624 | tf_op jit(solution)/shard_map/all_gather | solution.py:144
  770.0 6.7 multiply_convert_fusion.1
  781.3 6.6 multiply_reduce_fusion.8
  787.9 11.4 subtract_convert_fusion.2
  807.6 5.8 convolution_convert_fusion
  814.6 5.8 convolution_convert_fusion.2
  824.7 112.8 %all_gather.69 = f32[4096,16]{1,0:T(8,128)} all-gather(f32[128,16]{1,0:T(8,128)S(1)} %copy.133), channel_id=1, replica_groups=mesh['ctx'=16,'fsdp'=2] {'ctx','fsdp'}, dimensions={0}, use_global_device_ids=true | all-gather | bytes 270336 | tf_op jit(solution)/shard_map/all_gather | solution.py:183
  940.5 59.8 %all_gather.67 = f32[4096,16]{0,1:T(8,128)} all-gather(f32[128,16]{0,1:T(8,128)S(1)} %bitcast.239), channel_id=1, replica_groups=mesh['ctx'=16,'fsdp'=2] {'ctx','fsdp'}, dimensions={0}, use_global_device_ids=true | all-gather | bytes 270336 | tf_op jit(solution)/shard_map/all_gather | solution.py:182
  1001.2 122.1 %while.40 = (s32[]{:T(128)}, f32[128,16,128]{0,2,1:T(8,128)}, s32[8]{0:T(128)S(1)}, bf16[4096,2048]{0,1:T(8,128)(2,1)}, s32[4096]{0:T(1024)}, /*index=5*/s32[128...) while((s32[]{:T(128)}, f32[128,16,128]{0,2,1:T(8,128)}, ...), condition=%wide.region_12.13_spmd.clone, body=%wide.region_11.12_spmd.clone.sunk | while | flops 812187648 | bytes 26368728 | solution.py:207
  1010.7 6.2 fusion.148
  1025.7 6.3 fusion.148
  1040.8 6.4 fusion.148
  1056.0 6.6 fusion.148
  1071.3 6.3 fusion.148
  1086.4 6.6 fusion.148
  1101.8 6.3 fusion.148
  1117.0 6.3 fusion.148
  1125.6 7.0 convolution_convert_fusion.1
  1132.7 211.7 %while.41 = (s32[]{:T(128)}, f32[128,16,128]{0,2,1:T(8,128)}, f32[128,16,128]{0,2,1:T(8,128)}, s32[8]{0:T(128)S(1)}, bf16[4096,2048]{0,1:T(8,128)(2,1)}, /*index...) while((s32[]{:T(128)}, f32[128,16,128]{0,2,1:T(8,128)}, ...), condition=%wide.region_15.16_spmd.clone, body=%wide.region_14.15_spmd.clone.sunk | while | flops 1085341696 | bytes 39230184 | solution.py:234
  1152.8 6.1 fusion.157
  1179.0 6.2 fusion.157
  1199.8 5.6 fusion.158
  1205.4 6.3 fusion.157
  1226.2 6.1 fusion.158
  1232.3 6.2 fusion.157
  1258.6 6.2 fusion.157
  1279.4 5.7 fusion.158
  1285.1 6.4 fusion.157
  1311.6 6.2 fusion.157
  1338.1 6.3 fusion.157
  1365.5 56.6 %reduce-scatter.18.cloned.1.call-done = bf16[512,4096]{1,0:T(8,128)(2,1)} async-done(((bf16[1024,4096]{1,0:T(8,128)(2,1)}), bf16[512,4096]{1,0:T(8,128)(2,1)}) %reduce-scatter.18.cloned.1.call-update) | async-done | bytes 4194320 | tf_op jit(solution)/shard_map/reduce_scatter | solution.py:286
  1422.1 7.4 all-reduce.10
  1438.7 40.6 %reduce-scatter.10.cloned.1.call-done = bf16[512,2048]{0,1:T(8,128)(2,1)} async-done(((bf16[1024,2048]{0,1:T(8,128)(2,1)}), bf16[512,2048]{0,1:T(8,128)(2,1)}) %reduce-scatter.10.cloned.1.call-update) | async-done | bytes 2097168 | tf_op jit(solution)/shard_map/reduce_scatter | solution.py:274
  1479.3 57.1 %reduce-scatter.8.cloned.1.call-done = bf16[512,2048]{0,1:T(8,128)(2,1)} async-done(((bf16[1024,2048]{0,1:T(8,128)(2,1)}), bf16[512,2048]{0,1:T(8,128)(2,1)}) %reduce-scatter.8.cloned.1.call-update) | async-done | bytes 2097168 | tf_op jit(solution)/shard_map/reduce_scatter | solution.py:271
  1536.4 57.1 %reduce-scatter.12.cloned.1.call-done = bf16[512,2048]{0,1:T(8,128)(2,1)} async-done(((bf16[1024,2048]{0,1:T(8,128)(2,1)}), bf16[512,2048]{0,1:T(8,128)(2,1)}) %reduce-scatter.12.cloned.1.call-update) | async-done | bytes 2097168 | tf_op jit(solution)/shard_map/reduce_scatter | solution.py:277
  1593.6 877.7 %all-reduce.12 = (f32[512,2048]{0,1:T(8,128)}, f32[512,2048]{0,1:T(8,128)}, f32[512,2048]{0,1:T(8,128)}, f32[1024,1024]{1,0:T(8,128)}, f32[512,4096]{1,0:T(8,128...) all-reduce(bf16[512,2048]{0,1:T(8,128)(2,1)} %reduce-scatter.8.clon, ...), channel_id=1, replica_groups=mesh['ctx'=16,'fsdp'=2] {'ctx'}, use_global_device_ids=true, to_apply=%region_18.19 | all-reduce | flops 10488832 | bytes 62939136 | tf_op jit(solution)/shard_map/psum | solution.py:317
  (425 shorter events, 414.4 us)
Async XLA Ops:
  7.2 69.7 %copy-start.41 = (bf16[64]{0:T(256)(128)(2,1)S(1)}, bf16[64]{0:T(256)(128)(2,1)}, u32[]{:S(2)}) copy-start(bf16[64]{0:T(256)(128)(2,1)} %param.31) | copy-start | bytes 388
  7.2 69.9 %copy-start.42 = (bf16[64]{0:T(256)(128)(2,1)S(1)}, bf16[64]{0:T(256)(128)(2,1)}, u32[]{:S(2)}) copy-start(bf16[64]{0:T(256)(128)(2,1)} %param.30) | copy-start | bytes 388
  7.2 70.1 %copy-start.43 = (bf16[32]{0:T(256)(128)(2,1)S(1)}, bf16[32]{0:T(256)(128)(2,1)}, u32[]{:S(2)}) copy-start(bf16[32]{0:T(256)(128)(2,1)} %param.32) | copy-start | bytes 196
  7.2 70.4 %copy-start.44 = (bf16[32]{0:T(256)(128)(2,1)S(1)}, bf16[32]{0:T(256)(128)(2,1)}, u32[]{:S(2)}) copy-start(bf16[32]{0:T(256)(128)(2,1)} %param.33) | copy-start | bytes 196
  7.2 65.8 %all-gather.18.cloned.1.call-start = ((), (), s32[]{:S(2)}) async-start(), calls=%async_computation.10 | async-start | bytes 4325376 | tf_op jit(solution)/shard_map/all_gather | solution.py:92
  8.0 128.7 %all-gather.12.cloned.1.call-start = ((), (), s32[]{:S(2)}) async-start(), calls=%async_computation.7 | async-start | bytes 4325376 | tf_op jit(solution)/shard_map/all_gather | solution.py:91
  8.7 191.5 %all-gather.16.cloned.1.call-start = ((), (), s32[]{:S(2)}) async-start(), calls=%async_computation.9 | async-start | bytes 4325376 | tf_op jit(solution)/shard_map/all_gather | solution.py:90
  9.4 306.7 %all-gather.20.cloned.1.call-start = ((), (), s32[]{:S(2)}) async-start(), calls=%async_computation.11 | async-start | bytes 17301504 | tf_op jit(solution)/shard_map/all_gather | solution.py:115
  10.6 189.7 %copy-start.9 = (bf16[128,1024]{1,0:T(8,128)(2,1)}, bf16[128,1024]{1,0:T(8,128)(2,1)S(1)}, u32[]{:S(2)}) copy-start(bf16[128,1024]{1,0:T(8,128)(2,1)S(1)} %convert_element_type.172) | copy-start | bytes 786436
  76.8 387.7 %all-gather.14.cloned.1.call-start = ((), (), s32[]{:S(2)}) async-start(), calls=%async_computation.8 | async-start | bytes 17301504 | tf_op jit(solution)/shard_map/all_gather | solution.py:114
  117.9 22.4 copy-start.32
  117.9 85.9 %copy-start.30 = (f32[2048]{0:T(1024)}, f32[2048]{0:T(1024)S(1)}, u32[]{:S(2)}) copy-start(f32[2048]{0:T(1024)S(1)} %convert_element_type.177) | copy-start | bytes 24580
  118.9 86.0 %copy-start.26 = (f32[128,64]{0,1:T(8,128)}, f32[128,64]{0,1:T(8,128)S(1)}, u32[]{:S(2)}) copy-start(f32[128,64]{0,1:T(8,128)S(1)} %get-tuple-element.606) | copy-start | bytes 98308
  118.9 86.0 %copy-start.28 = (f32[128,64]{0,1:T(8,128)}, f32[128,64]{0,1:T(8,128)S(1)}, u32[]{:S(2)}) copy-start(f32[128,64]{0,1:T(8,128)S(1)} %get-tuple-element.607) | copy-start | bytes 98308
  206.1 370.6 %all-gather.22.cloned.1.call-start = ((), (), s32[]{:S(2)}) async-start(), calls=%async_computation.12 | async-start | bytes 4325376 | tf_op jit(solution)/shard_map/all_gather | solution.py:93
  206.6 399.9 %all-gather.24.cloned.1.call-start = ((), (), s32[]{:S(2)}) async-start(), calls=%async_computation.13 | async-start | bytes 8650752 | tf_op jit(solution)/shard_map/all_gather | solution.py:142
  207.4 477.9 %all-gather.26.cloned.1.call-start = ((), (), s32[]{:S(2)}) async-start(), calls=%async_computation.14 | async-start | bytes 8650752 | tf_op jit(solution)/shard_map/all_gather | solution.py:143
  208.1 555.9 %all-gather.28.cloned.1.call-start = ((), (), s32[]{:S(2)}) async-start(), calls=%async_computation.15 | async-start | bytes 8650752 | tf_op jit(solution)/shard_map/all_gather | solution.py:144
  208.9 923.8 %all-gather.30.cloned.1.call-start = ((), (), s32[]{:S(2)}) async-start(), calls=%async_computation.16 | async-start | bytes 17301504 | tf_op jit(solution)/shard_map/all_gather | solution.py:208
  209.8 922.9 %all-gather.32.cloned.1.call-start = ((), (), s32[]{:S(2)}) async-start(), calls=%async_computation.17 | async-start | bytes 17301504 | tf_op jit(solution)/shard_map/all_gather | solution.py:209
  485.8 5.0 copy-start
  499.6 5.0 copy-start
  513.4 5.0 copy-start
  527.2 5.0 copy-start
  541.1 5.0 copy-start
  554.9 5.2 copy-start
  568.9 5.0 copy-start
  575.2 5.4 copy-start.12
  764.0 4.9 copy-start.14
  764.0 6.0 copy-start.1
  769.7 7.0 slice-start
  769.9 6.8 copy-start.24
  770.0 6.7 slice-start.1
  781.2 6.6 copy-start.13
  781.3 18.8 copy-start.4
  787.9 11.4 copy-start.17
  802.4 563.1 %reduce-scatter.14.cloned.1.call-start = ((), (), s32[]{:S(2)}) async-start(), calls=%async_computation.21 | async-start | bytes 6291456 | tf_op jit(solution)/shard_map/reduce_scatter | solution.py:280
  806.7 558.8 %reduce-scatter.20.cloned.1.call-start = ((), (), s32[]{:S(2)}) async-start(), calls=%async_computation.24 | async-start | bytes 12582912 | tf_op jit(solution)/shard_map/reduce_scatter | solution.py:289
  813.4 552.1 %reduce-scatter.16.cloned.1.call-start = ((), (), s32[]{:S(2)}) async-start(), calls=%async_computation.22 | async-start | bytes 12582912 | tf_op jit(solution)/shard_map/reduce_scatter | solution.py:283
  820.4 601.7 %reduce-scatter.18.cloned.1.call-start = ((), (), s32[]{:S(2)}) async-start(), calls=%async_computation.23 | async-start | bytes 12582912 | tf_op jit(solution)/shard_map/reduce_scatter | solution.py:286
  1132.6 346.7 %reduce-scatter.10.cloned.1.call-start = ((), (), s32[]{:S(2)}) async-start(), calls=%async_computation.19 | async-start | bytes 6291456 | tf_op jit(solution)/shard_map/reduce_scatter | solution.py:274
  1132.7 213.0 %copy-start.27 = (f32[128,64]{0,1:T(8,128)S(1)}, f32[128,64]{0,1:T(8,128)}, u32[]{:S(2)}) copy-start(f32[128,64]{0,1:T(8,128)} %copy-done.26) | copy-start | bytes 98308
  1132.7 213.0 %copy-start.29 = (f32[128,64]{0,1:T(8,128)S(1)}, f32[128,64]{0,1:T(8,128)}, u32[]{:S(2)}) copy-start(f32[128,64]{0,1:T(8,128)} %copy-done.28) | copy-start | bytes 98308
  1352.7 183.7 %reduce-scatter.8.cloned.1.call-start = ((), (), s32[]{:S(2)}) async-start(), calls=%async_computation.18 | async-start | bytes 6291456 | tf_op jit(solution)/shard_map/reduce_scatter | solution.py:271
  1358.4 235.2 %reduce-scatter.12.cloned.1.call-start = ((), (), s32[]{:S(2)}) async-start(), calls=%async_computation.20 | async-start | bytes 6291456 | tf_op jit(solution)/shard_map/reduce_scatter | solution.py:277
  1362.9 59.2 %copy-start.34 = (bf16[1024]{0:T(1024)(128)(2,1)S(1)}, bf16[1024]{0:T(1024)(128)(2,1)}, u32[]{:S(2)}) copy-start(bf16[1024]{0:T(1024)(128)(2,1)} %get-tuple-element.489) | copy-start | bytes 6148
  1362.9 66.7 %copy-start.18 = (f32[128,1024]{1,0:T(8,128)S(1)}, f32[128,1024]{1,0:T(8,128)}, u32[]{:S(2)}) copy-start(f32[128,1024]{1,0:T(8,128)} %copy-done.17) | copy-start | bytes 1572868
  1436.4 157.2 %copy-start.22 = (bf16[1024,1024]{1,0:T(8,128)(2,1)S(1)}, bf16[1024,1024]{1,0:T(8,128)(2,1)}, u32[]{:S(2)}) copy-start(bf16[1024,1024]{1,0:T(8,128)(2,1)} %reduce-scatter.14.cloned.1.call-done) | copy-start | bytes 6291460
  (25 other events, 43.3 us)
Sparse Core Ops, SparseCore 0:
  11.0 61.9 all-gather.17
  76.0 60.5 all-gather.11
  139.6 60.5 all-gather.15
  203.1 112.9 all-gather.19
  319.4 145.0 all-gather.13
  467.3 59.9 all-gather.21
  530.3 76.1 all-gather.23
  609.5 75.6 all-gather.25
  688.3 75.7 all-gather.27
  766.8 172.4 all-gather.29
  942.3 117.0 all-gather.31
  1062.1 53.6 reduce-scatter.13
  1118.6 99.3 reduce-scatter.19
  1220.7 99.3 reduce-scatter.15
  1322.7 99.3 reduce-scatter.17
  1424.8 54.4 reduce-scatter.9
  1482.0 54.3 reduce-scatter.7
  1539.1 54.3 reduce-scatter.11
where the time goes:
time: 2510 us; the launch traced here: 2490 us
  blocking collectives  1100 us (44%)
  waiting for transfers between devices  758 us (30%)
  matrix products  348 us (14%)
  local copies, waits for them, and re-layouts  216 us (9%)
  other arithmetic  39.9 us (2%)
    psum x1, blocking collectives, per_device(): lax.psum((share_wq, share_wk, share_wv, share_wo, share_wg, share_wu, sha...  878 us
    all_gather x1, waiting for transfers between devices, per_device(): keys_in = lax.all_gather(key, ('ctx', 'fsdp'), axis=0, tiled=True)  128 us
    all_gather x1, blocking collectives, per_device(): lax.all_gather(delta_rows, ('ctx', 'fsdp'), axis=0, tiled=True)  113 us
    all_gather x1, waiting for transfers between devices, per_device(): values_in = lax.all_gather(value, ('ctx', 'fsdp'), axis=0, tiled=True)  105 us
    all_gather x1, waiting for transfers between devices, per_device(): lax.all_gather(w_up, ('ctx', 'fsdp'), axis=0, tiled=True)  72.7 us
    all_gather x1, waiting for transfers between devices, per_device(): lax.all_gather(w_down, ('ctx', 'fsdp'), axis=0, tiled=True)  71.9 us
    all_gather x1, waiting for transfers between devices, per_device(): lax.all_gather(w_value, ('ctx', 'fsdp'), axis=0, tiled=True)  62.4 us
    all_gather x1, blocking collectives, per_device(): lax.all_gather(lse.T, ('ctx', 'fsdp'), axis=0, tiled=True)  59.8 us
  transfers between devices with their start and end apart: 18, of which 12 were waited for; matrix products, arithmetic and copies ran while one was open for 23% of the time, Pallas kernels for 0%

commit v1 on v0

--- a/solution.py
+++ b/solution.py
@@ -111,8 +111,11 @@
         jnp.zeros((heads, rows), f32),
         jnp.zeros((rows, heads, head_size), f32),
     )
-    keys_in = lax.all_gather(key, ("ctx", "fsdp"), axis=0, tiled=True)
-    values_in = lax.all_gather(value, ("ctx", "fsdp"), axis=0, tiled=True)
+    keys_in, values_in = jnp.split(
+        lax.all_gather(jnp.concatenate([key, value], axis=1), ("ctx", "fsdp"), axis=0, tiled=True),
+        [key.shape[1]],
+        axis=1,
+    )
     count = keys_in.shape[0]
     size = block_size()
 

time: 2510 us -> 2670 us (1.064)
  local copies, waits for them, and re-layouts: 216 us -> 348 us
    reduce_scatter x1, waiting for transfers between devices: 0.02 us -> 102 us  [per_device(): lax.psum_scatter(local_wd.astype(jnp.bfloat16), 'fsdp', scatter_dimension...]
    all_gather x1, waiting for transfers between devices: 72.7 us -> 0.01 us  [per_device(): lax.all_gather(w_up, ('ctx', 'fsdp'), axis=0, tiled=True)]
    all_gather x1, waiting for transfers between devices: 0.02 us -> 71 us  [per_device(): cotangents_in = lax.all_gather(d_att, ('ctx', 'fsdp'), axis=0, tiled=True)]
    dynamic_slice x0 -> x16, local copies, waits for them, and re-layouts: none -> 54.6 us  [the longest x8 31.4 us: attend_step(): lax.dynamic_slice_in_dim(keys_in, low, size).reshape(size, heads, head_size)]
    all_gather x1, waiting for transfers between devices: 59 us -> 16.7 us  [per_device(): lax.all_gather(w_query, ('ctx', 'fsdp'), axis=0, tiled=True)]
    all_gather x1, waiting for transfers between devices: 17.7 us -> 58.9 us  [per_device(): lax.all_gather(w_key, ('ctx', 'fsdp'), axis=0, tiled=True)]
    dynamic_slice x8 -> x16, local copies, waits for them, and re-layouts: 30.8 us -> 70.1 us  [query_step(): lax.dynamic_slice_in_dim(query_values_in, low, query_size)]
    dynamic_slice x8 -> x16, local copies, waits for them, and re-layouts: 20.2 us -> 52.5 us  [attend_step(): lax.dynamic_slice_in_dim(values_in, low, size)]
  transfers between devices with their start and end apart: 18 -> 19, of which waited for: 12 -> 12; matrix products, arithmetic and copies ran while one was open for 23% -> 28% of each run, Pallas kernels for 0% -> 0%
where the time goes in v1:
time: 2670 us; the launch traced here: 2650 us
  blocking collectives  1090 us (41%)
  waiting for transfers between devices  767 us (29%)
  matrix products  359 us (13%)
  local copies, waits for them, and re-layouts  348 us (13%)
  other arithmetic  58.3 us (2%)
    psum x1, blocking collectives, per_device(): lax.psum((share_wq, share_wk, share_wv, share_wo, share_wg, share_wu, sha...  878 us
    all_gather x1, waiting for transfers between devices, per_device(): lax.all_gather(jnp.concatenate([key, value], axis=1), ('ctx', 'fsdp'), ax...  187 us
    reduce_scatter x1, waiting for transfers between devices, per_device(): lax.psum_scatter(local_wd.astype(jnp.bfloat16), 'fsdp', scatter_dimension...  102 us
    all_gather x1, blocking collectives, per_device(): lax.all_gather(delta_rows, ('ctx', 'fsdp'), axis=0, tiled=True)  97.9 us
    all_gather x1, waiting for transfers between devices, per_device(): cotangents_in = lax.all_gather(d_att, ('ctx', 'fsdp'), axis=0, tiled=True)  71 us
    dynamic_slice x16, local copies, waits for them, and re-layouts, query_step(): lax.dynamic_slice_in_dim(query_values_in, low, query_size)  70.1 us
    all_gather x1, blocking collectives, per_device(): lax.all_gather(lse.T, ('ctx', 'fsdp'), axis=0, tiled=True)  61.8 us
    all_gather x1, waiting for transfers between devices, per_device(): lax.all_gather(w_key, ('ctx', 'fsdp'), axis=0, tiled=True)  58.9 us
  transfers between devices with their start and end apart: 19, of which 12 were waited for; matrix products, arithmetic and copies ran while one was open for 28% of the time, Pallas kernels for 0%

profile of v1, /device:TPU:20, one launch (start us, length us, event | category | flops | bytes accessed | tf_op | source)
XLA Modules:
  0.0 2651.8 jit_solution(6921764213464491818)
XLA Ops:
  14.0 41.3 %all-reduce.9 = (bf16[2048]{0:T(1024)(128)(2,1)S(1)}, bf16[2048]{0:T(1024)(128)(2,1)S(1)}, bf16[1024]{0:T(1024)(128)(2,1)S(1)}, bf16[1024]{0:T(1024)(128)(2,1)S(1)}) all-reduce(bf16[2048]{0:T(1024)(128)(2,1)S(1)} %dynamic-update-slice, bf16[2048]{0:T(1024)(128)(2,1)S(1)} %dynamic-update-slice.1, ...), channel_id=1, replica_groups=mesh['ctx'=16,'fsdp'=2] {'ctx','fsdp'}, use_global_device_ids=true, to_apply=%add | all-reduce | flops 6144 | bytes 24576
  56.3 16.7 all-gather.19.cloned.1.call-done
  77.6 58.9 %all-gather.13.cloned.1.call-done = bf16[1024,2048]{1,0:T(8,128)(2,1)} async-done(((bf16[32,2048]{1,0:T(8,128)(2,1)}), bf16[1024,2048]{1,0:T(8,128)(2,1)}) %all-gather.13.cloned.1.call-update) | async-done | bytes 4194320 | tf_op jit(solution)/shard_map/all_gather | solution.py:91
  142.3 57.8 %all-gather.15.cloned.1.call-done = bf16[1024,2048]{1,0:T(8,128)(2,1)} async-done(((bf16[32,2048]{1,0:T(8,128)(2,1)}), bf16[1024,2048]{1,0:T(8,128)(2,1)}) %all-gather.15.cloned.1.call-update) | async-done | bytes 4194320 | tf_op jit(solution)/shard_map/all_gather | solution.py:92
  210.5 186.7 %all-gather.17.cloned.1.call-done = bf16[4096,4096]{1,0:T(8,128)(2,1)} async-done(((bf16[128,4096]{1,0:T(8,128)(2,1)}), bf16[4096,4096]{1,0:T(8,128)(2,1)}) %all-gather.17.cloned.1.call-update) | async-done | bytes 33554448 | tf_op jit(solution)/shard_map/all_gather | solution.py:115
  397.1 23.6 fusion.46
  420.8 207.9 %while.39 = (s32[]{:T(128)}, f32[16,128]{1,0:T(8,128)S(1)}, f32[16,128]{1,0:T(8,128)S(1)}, f32[128,16,128]{0,2,1:T(8,128)}, s32[8]{0:T(128)S(1)}, /*index=5*/s32...) while((s32[]{:T(128)}, f32[16,128]{1,0:T(8,128)S(1)}, ...), condition=%wide.region_5.6_spmd.clone, body=%wide.region_2.5_spmd.clone.sunk | while | flops 551366656 | bytes 36575960 | solution.py:140
  441.3 5.7 fusion.142
  633.4 6.0 fusion.49
  639.4 6.9 multiply_convert_fusion.3
  646.3 50.4 %all-gather.27.cloned.1.call-done = bf16[4096,1024]{1,0:T(8,128)(2,1)} async-done(((bf16[128,1024]{1,0:T(8,128)(2,1)}), bf16[4096,1024]{1,0:T(8,128)(2,1)}) %all-gather.27.cloned.1.call-update) | async-done | bytes 8388624 | tf_op jit(solution)/shard_map/all_gather | solution.py:147
  702.6 5.7 multiply_convert_fusion.1
  711.2 7.2 multiply_reduce_fusion.8
  718.4 11.8 subtract_convert_fusion.2
  738.7 5.8 convolution_convert_fusion.2
  744.6 5.8 convolution_convert_fusion.1
  754.7 97.9 %all_gather.71 = f32[4096,16]{1,0:T(8,128)} all-gather(f32[128,16]{1,0:T(8,128)S(1)} %copy.145), channel_id=1, replica_groups=mesh['ctx'=16,'fsdp'=2] {'ctx','fsdp'}, dimensions={0}, use_global_device_ids=true | all-gather | bytes 270336 | tf_op jit(solution)/shard_map/all_gather | solution.py:186
  855.5 61.8 %all_gather.69 = f32[4096,16]{0,1:T(8,128)} all-gather(f32[128,16]{0,1:T(8,128)S(1)} %bitcast.239), channel_id=1, replica_groups=mesh['ctx'=16,'fsdp'=2] {'ctx','fsdp'}, dimensions={0}, use_global_device_ids=true | all-gather | bytes 270336 | tf_op jit(solution)/shard_map/all_gather | solution.py:185
  918.3 34.6 %all-gather.31.cloned.1.call-done = bf16[4096,2048]{1,0:T(8,128)(2,1)} async-done(((bf16[128,2048]{1,0:T(8,128)(2,1)}), bf16[4096,2048]{1,0:T(8,128)(2,1)}) %all-gather.31.cloned.1.call-update) | async-done | bytes 16777232 | tf_op jit(solution)/shard_map/all_gather | solution.py:190
  952.9 183.5 %while.40 = (s32[]{:T(128)}, f32[128,16,128]{0,2,1:T(8,128)}, s32[8]{0:T(128)S(1)}, bf16[4096,2048]{1,0:T(8,128)(2,1)}, s32[4096]{0:T(1024)}, /*index=5*/s32[128...) while((s32[]{:T(128)}, f32[128,16,128]{0,2,1:T(8,128)}, ...), condition=%wide.region_12.13_spmd.clone, body=%wide.region_11.12_spmd.clone.sunk | while | flops 812187648 | bytes 34757344 | solution.py:210
  969.5 6.1 fusion.149
  992.2 6.3 fusion.149
  1015.1 6.3 fusion.149
  1038.2 6.4 fusion.149
  1061.1 6.3 fusion.149
  1084.0 6.5 fusion.149
  1107.2 6.3 fusion.149
  1130.1 6.3 fusion.149
  1138.8 7.0 convolution_convert_fusion
  1145.9 71.0 %all-gather.35.cloned.1.call-done = bf16[4096,2048]{1,0:T(8,128)(2,1)} async-done(((bf16[128,2048]{1,0:T(8,128)(2,1)}), bf16[4096,2048]{1,0:T(8,128)(2,1)}) %all-gather.35.cloned.1.call-update) | async-done | bytes 16777232 | tf_op jit(solution)/shard_map/all_gather | solution.py:212
  1216.9 211.3 %while.41 = (s32[]{:T(128)}, f32[128,16,128]{0,2,1:T(8,128)}, f32[128,16,128]{0,2,1:T(8,128)}, s32[8]{0:T(128)S(1)}, bf16[4096,2048]{0,1:T(8,128)(2,1)}, /*index...) while((s32[]{:T(128)}, f32[128,16,128]{0,2,1:T(8,128)}, ...), condition=%wide.region_15.16_spmd.clone, body=%wide.region_14.15_spmd.clone.sunk | while | flops 1085341696 | bytes 39230192 | solution.py:237
  1231.7 6.2 fusion.158
  1258.0 6.2 fusion.158
  1284.2 6.2 fusion.158
  1290.4 5.7 fusion.159
  1310.9 6.2 fusion.158
  1317.1 5.7 fusion.159
  1337.5 6.2 fusion.158
  1363.7 6.3 fusion.158
  1390.2 6.2 fusion.158
  1416.6 6.2 fusion.158
  1449.4 28.1 %reduce-scatter.18.cloned.1.call-done = bf16[512,4096]{1,0:T(8,128)(2,1)} async-done(((bf16[1024,4096]{1,0:T(8,128)(2,1)}), bf16[512,4096]{1,0:T(8,128)(2,1)}) %reduce-scatter.18.cloned.1.call-update) | async-done | bytes 4194320 | tf_op jit(solution)/shard_map/reduce_scatter | solution.py:289
  1477.5 102.1 %reduce-scatter.20.cloned.1.call-done = bf16[2048,1024]{1,0:T(8,128)(2,1)} async-done(((bf16[4096,1024]{1,0:T(8,128)(2,1)}), bf16[2048,1024]{1,0:T(8,128)(2,1)}) %reduce-scatter.20.cloned.1.call-update) | async-done | bytes 4194320 | tf_op jit(solution)/shard_map/reduce_scatter | solution.py:292
  1579.6 7.4 all-reduce.10
  1596.2 40.5 %reduce-scatter.8.cloned.1.call-done = bf16[512,2048]{0,1:T(8,128)(2,1)} async-done(((bf16[1024,2048]{0,1:T(8,128)(2,1)}), bf16[512,2048]{0,1:T(8,128)(2,1)}) %reduce-scatter.8.cloned.1.call-update) | async-done | bytes 2097168 | tf_op jit(solution)/shard_map/reduce_scatter | solution.py:274
  1636.7 57.1 %reduce-scatter.10.cloned.1.call-done = bf16[512,2048]{0,1:T(8,128)(2,1)} async-done(((bf16[1024,2048]{0,1:T(8,128)(2,1)}), bf16[512,2048]{0,1:T(8,128)(2,1)}) %reduce-scatter.10.cloned.1.call-update) | async-done | bytes 2097168 | tf_op jit(solution)/shard_map/reduce_scatter | solution.py:277
  1693.9 57.3 %reduce-scatter.12.cloned.1.call-done = bf16[512,2048]{0,1:T(8,128)(2,1)} async-done(((bf16[1024,2048]{0,1:T(8,128)(2,1)}), bf16[512,2048]{0,1:T(8,128)(2,1)}) %reduce-scatter.12.cloned.1.call-update) | async-done | bytes 2097168 | tf_op jit(solution)/shard_map/reduce_scatter | solution.py:280
  1751.1 877.7 %all-reduce.12 = (f32[512,2048]{0,1:T(8,128)}, f32[512,2048]{0,1:T(8,128)}, f32[512,2048]{0,1:T(8,128)}, f32[1024,1024]{1,0:T(8,128)}, f32[512,4096]{1,0:T(8,128...) all-reduce(bf16[512,2048]{0,1:T(8,128)(2,1)} %reduce-scatter.8.clon, ...), channel_id=1, replica_groups=mesh['ctx'=16,'fsdp'=2] {'ctx'}, use_global_device_ids=true, to_apply=%region_18.19 | all-reduce | flops 10488832 | bytes 62939136 | tf_op jit(solution)/shard_map/psum | solution.py:320
  (448 shorter events, 574.0 us)
Async XLA Ops:
  7.2 65.8 %all-gather.19.cloned.1.call-start = ((), (), s32[]{:S(2)}) async-start(), calls=%async_computation.10 | async-start | bytes 4325376 | tf_op jit(solution)/shard_map/all_gather | solution.py:90
  7.9 128.6 %all-gather.13.cloned.1.call-start = ((), (), s32[]{:S(2)}) async-start(), calls=%async_computation.7 | async-start | bytes 4325376 | tf_op jit(solution)/shard_map/all_gather | solution.py:91
  8.7 191.4 %all-gather.15.cloned.1.call-start = ((), (), s32[]{:S(2)}) async-start(), calls=%async_computation.8 | async-start | bytes 4325376 | tf_op jit(solution)/shard_map/all_gather | solution.py:92
  9.4 387.7 %all-gather.17.cloned.1.call-start = ((), (), s32[]{:S(2)}) async-start(), calls=%async_computation.9 | async-start | bytes 34603008 | tf_op jit(solution)/shard_map/all_gather | solution.py:115
  10.5 189.5 %copy-start.8 = (bf16[128,1024]{1,0:T(8,128)(2,1)}, bf16[128,1024]{1,0:T(8,128)(2,1)S(1)}, u32[]{:S(2)}) copy-start(bf16[128,1024]{1,0:T(8,128)(2,1)S(1)} %convert_element_type.172) | copy-start | bytes 786436
  55.3 21.3 copy-start.35
  55.3 84.8 %copy-start.33 = (f32[2048]{0:T(1024)}, f32[2048]{0:T(1024)S(1)}, u32[]{:S(2)}) copy-start(f32[2048]{0:T(1024)S(1)} %convert_element_type.173) | copy-start | bytes 24580
  56.3 84.8 %copy-start.29 = (f32[128,64]{0,1:T(8,128)}, f32[128,64]{0,1:T(8,128)S(1)}, u32[]{:S(2)}) copy-start(f32[128,64]{0,1:T(8,128)S(1)} %get-tuple-element.608) | copy-start | bytes 98308
  56.3 84.8 %copy-start.31 = (f32[128,64]{0,1:T(8,128)}, f32[128,64]{0,1:T(8,128)S(1)}, u32[]{:S(2)}) copy-start(f32[128,64]{0,1:T(8,128)S(1)} %get-tuple-element.609) | copy-start | bytes 98308
  141.7 63.6 %copy-start.21 = (bf16[128,2048]{1,0:T(8,128)(2,1)}, bf16[128,2048]{1,0:T(8,128)(2,1)S(1)}, u32[]{:S(2)}) copy-start(bf16[128,2048]{1,0:T(8,128)(2,1)S(1)} %copy.135) | copy-start | bytes 1572868
  203.0 4.6 copy-start.12
  204.1 426.1 %all-gather.21.cloned.1.call-start = ((), (), s32[]{:S(2)}) async-start(), calls=%async_computation.11 | async-start | bytes 4325376 | tf_op jit(solution)/shard_map/all_gather | solution.py:93
  204.7 428.7 %all-gather.23.cloned.1.call-start = ((), (), s32[]{:S(2)}) async-start(), calls=%async_computation.12 | async-start | bytes 8650752 | tf_op jit(solution)/shard_map/all_gather | solution.py:145
  205.3 434.1 %all-gather.25.cloned.1.call-start = ((), (), s32[]{:S(2)}) async-start(), calls=%async_computation.13 | async-start | bytes 8650752 | tf_op jit(solution)/shard_map/all_gather | solution.py:146
  206.1 490.6 %all-gather.27.cloned.1.call-start = ((), (), s32[]{:S(2)}) async-start(), calls=%async_computation.14 | async-start | bytes 8650752 | tf_op jit(solution)/shard_map/all_gather | solution.py:147
  206.8 711.5 %all-gather.29.cloned.1.call-start = ((), (), s32[]{:S(2)}) async-start(), calls=%async_computation.15 | async-start | bytes 17301504 | tf_op jit(solution)/shard_map/all_gather | solution.py:189
  207.5 745.4 %all-gather.31.cloned.1.call-start = ((), (), s32[]{:S(2)}) async-start(), calls=%async_computation.16 | async-start | bytes 17301504 | tf_op jit(solution)/shard_map/all_gather | solution.py:190
  208.1 937.7 %all-gather.33.cloned.1.call-start = ((), (), s32[]{:S(2)}) async-start(), calls=%async_computation.17 | async-start | bytes 17301504 | tf_op jit(solution)/shard_map/all_gather | solution.py:211
  209.0 1007.9 %all-gather.35.cloned.1.call-start = ((), (), s32[]{:S(2)}) async-start(), calls=%async_computation.18 | async-start | bytes 17301504 | tf_op jit(solution)/shard_map/all_gather | solution.py:212
  628.7 4.5 copy-start.14
  646.3 55.2 %copy-start.10 = (bf16[128,4096]{1,0:T(8,128)(2,1)}, bf16[128,4096]{1,0:T(8,128)(2,1)S(1)}, u32[]{:S(2)}) copy-start(bf16[128,4096]{1,0:T(8,128)(2,1)S(1)} %get-tuple-element.624) | copy-start | bytes 3145732
  696.6 4.9 copy-start.16
  696.6 6.0 copy-start
  702.3 6.0 slice-start
  702.5 5.8 copy-start.27
  702.6 5.7 slice-start.1
  708.3 2.9 copy-start.22
  711.2 7.2 copy-start.15
  711.2 19.7 copy-start.3
  718.4 11.8 copy-start.19
  733.3 716.1 %reduce-scatter.14.cloned.1.call-start = ((), (), s32[]{:S(2)}) async-start(), calls=%async_computation.22 | async-start | bytes 6291456 | tf_op jit(solution)/shard_map/reduce_scatter | solution.py:283
  737.5 711.8 %reduce-scatter.16.cloned.1.call-start = ((), (), s32[]{:S(2)}) async-start(), calls=%async_computation.23 | async-start | bytes 12582912 | tf_op jit(solution)/shard_map/reduce_scatter | solution.py:286
  744.5 733.0 %reduce-scatter.18.cloned.1.call-start = ((), (), s32[]{:S(2)}) async-start(), calls=%async_computation.24 | async-start | bytes 12582912 | tf_op jit(solution)/shard_map/reduce_scatter | solution.py:289
  750.4 2.3 copy-start.11
  750.4 829.2 %reduce-scatter.20.cloned.1.call-start = ((), (), s32[]{:S(2)}) async-start(), calls=%async_computation.25 | async-start | bytes 12582912 | tf_op jit(solution)/shard_map/reduce_scatter | solution.py:292
  952.9 185.9 %copy-start.28 = (bf16[128,1024]{1,0:T(8,128)(2,1)S(1)}, bf16[128,1024]{1,0:T(8,128)(2,1)}, u32[]{:S(2)}) copy-start(bf16[128,1024]{1,0:T(8,128)(2,1)} %copy-done.27) | copy-start | bytes 786436
  1145.8 490.9 %reduce-scatter.8.cloned.1.call-start = ((), (), s32[]{:S(2)}) async-start(), calls=%async_computation.19 | async-start | bytes 6291456 | tf_op jit(solution)/shard_map/reduce_scatter | solution.py:274
  1216.9 212.7 %copy-start.30 = (f32[128,64]{0,1:T(8,128)S(1)}, f32[128,64]{0,1:T(8,128)}, u32[]{:S(2)}) copy-start(f32[128,64]{0,1:T(8,128)} %copy-done.29) | copy-start | bytes 98308
  1216.9 212.7 %copy-start.32 = (f32[128,64]{0,1:T(8,128)S(1)}, f32[128,64]{0,1:T(8,128)}, u32[]{:S(2)}) copy-start(f32[128,64]{0,1:T(8,128)} %copy-done.31) | copy-start | bytes 98308
  1436.6 2.0 copy-start.43
  1436.6 257.3 %reduce-scatter.10.cloned.1.call-start = ((), (), s32[]{:S(2)}) async-start(), calls=%async_computation.20 | async-start | bytes 6291456 | tf_op jit(solution)/shard_map/reduce_scatter | solution.py:277
  1442.3 308.9 %reduce-scatter.12.cloned.1.call-start = ((), (), s32[]{:S(2)}) async-start(), calls=%async_computation.21 | async-start | bytes 6291456 | tf_op jit(solution)/shard_map/reduce_scatter | solution.py:280
  1446.8 132.8 %copy-start.37 = (bf16[1024]{0:T(1024)(128)(2,1)S(1)}, bf16[1024]{0:T(1024)(128)(2,1)}, u32[]{:S(2)}) copy-start(bf16[1024]{0:T(1024)(128)(2,1)} %get-tuple-element.489) | copy-start | bytes 6148
  1446.8 132.8 %copy-start.38 = (bf16[1024]{0:T(1024)(128)(2,1)S(1)}, bf16[1024]{0:T(1024)(128)(2,1)}, u32[]{:S(2)}) copy-start(bf16[1024]{0:T(1024)(128)(2,1)} %get-tuple-element.491) | copy-start | bytes 6148
  1446.8 140.3 %copy-start.20 = (f32[128,1024]{1,0:T(8,128)S(1)}, f32[128,1024]{1,0:T(8,128)}, u32[]{:S(2)}) copy-start(f32[128,1024]{1,0:T(8,128)} %copy-done.19) | copy-start | bytes 1572868
  1586.9 4.7 copy-start.1
  1591.7 2.2 copy-start.2
  1593.9 157.3 %copy-start.25 = (bf16[1024,1024]{1,0:T(8,128)(2,1)S(1)}, bf16[1024,1024]{1,0:T(8,128)(2,1)}, u32[]{:S(2)}) copy-start(bf16[1024,1024]{1,0:T(8,128)(2,1)} %reduce-scatter.14.cloned.1.call-done) | copy-start | bytes 6291460
  (19 other events, 22.6 us)
Sparse Core Ops, SparseCore 0:
  11.0 61.9 all-gather.18
  76.0 60.4 all-gather.12
  139.5 60.4 all-gather.14
  204.3 192.8 all-gather.16
  400.0 60.0 all-gather.20
  462.9 76.2 all-gather.22
  542.1 75.7 all-gather.24
  620.9 75.6 all-gather.26
  699.6 132.2 all-gather.28
  834.8 118.0 all-gather.30
  956.4 145.1 all-gather.32
  1104.4 112.4 all-gather.34
  1219.8 53.5 reduce-scatter.13
  1276.1 99.2 reduce-scatter.15
  1378.1 99.3 reduce-scatter.17
  1480.2 99.3 reduce-scatter.19
  1582.3 54.3 reduce-scatter.7
  1639.5 54.3 reduce-scatter.9
  1696.7 54.3 reduce-scatter.11
